TPU v7x, 128 devices: a whole 4x4x4 slice. The times are simulated.
128 devices in a mesh: orow: 16 (over z, x), ocol: 8 (over y, core).
Axes of the slice: x: 4, y: 4, z: 4, core: 2. Of those that a mesh axis runs over, the one named last changes fastest.
Arguments:
- integrals: bfloat16 [2304, 32, 384], P('ocol', 'orow'), may hold values from -0.29882812 to 0.29882812
- occ_count: int32 [16], replicated, may hold values from 1 to 2
- occ_energy: float32 [32], replicated, may hold values from -2 to -0.5
- vir_energy: float32 [384], replicated, may hold values from 0.3 to 2.5
- task_iblock: int32 [64, 1], replicated, may hold values from 0 to 15; in each aligned block of 64 rows (0 to 63, 64 to 127, ...) at most 8 rows name the same one
- task_jblock: int32 [64], replicated, may hold values from 0 to 15
Outputs:
- gamma_out: float32 [2304, 32, 384], P('ocol', 'orow')
- density: float32 [384, 384], replicated
Inputs may be any that keep to these rules, and one draw needn't show every extreme that they name: `task_iblock`: no first block is named by more than 8 tasks, and some first block by exactly 8.
All inputs are finite; a program needn't handle non-finite values.
Results may differ from a plain program's by a relative error of at most 0.0019.
Values may be sent and summed in bfloat16 or wider, within the bound.
No kernel may reach another device: no remote copies, remote signals or barrier semaphores. Data moves between devices by JAX's collectives and lax.ppermute only.
A program may use at most 128 MiB of HBM per device.

v0:
```python
import jax
import jax.numpy as jnp
from jax import lax
from jax.sharding import Mesh
from jax.sharding import PartitionSpec as P

OROW = ("orow_0", "orow_1")
OCOL = ("ocol_0", "ocol_1")
OROW_OCOL = ("orow_0", "orow_1", "ocol_0", "ocol_1")


def rows_for(lines, length):
    spare = -lines.shape[0] % length
    if not spare:
        return lines
    return jnp.concatenate([lines, jnp.zeros((spare, *lines.shape[1:]), lines.dtype)])


def sum_in_order(pieces, axes, turns):
    lengths = [lax.axis_size(a) for a in axes]
    pieces = pieces.reshape(*lengths, *pieces.shape[1:])
    pieces = pieces.transpose(*turns, *range(len(axes), pieces.ndim))
    pieces = pieces.reshape(-1, *pieces.shape[len(axes) :])
    for k in turns:
        pieces = lax.psum_scatter(pieces, axes[k], scatter_dimension=0, tiled=True)
    return pieces[0]


def gather_in_order(x, axes, turns):
    pieces = x
    for k in turns:
        pieces = lax.all_gather(pieces, axes[k])
    done = turns[::-1]
    back = [done.index(k) for k in range(len(axes))]
    pieces = pieces.transpose(*back, *range(len(axes), pieces.ndim))
    return pieces.reshape(-1, *x.shape)


def total_of(x, axes, turns):
    length, lines = (lax.axis_size(axes), x.reshape(-1, *x.shape[1:][-1:]))
    pieces = rows_for(lines, length).reshape(length, -1, *lines.shape[1:])
    own = sum_in_order(pieces, axes, turns)
    whole = gather_in_order(own, axes, turns[::-1]).reshape(-1, *lines.shape[1:])
    return whole[: len(lines)].reshape(x.shape)


def make_amplitudes(k_total, i_energy, j_energy, vir_energy, usable):
    slots = k_total.shape[0]
    orbitals = i_energy.shape[1]
    virtuals = vir_energy.shape[0]
    k_grid = k_total.reshape(slots, orbitals, virtuals, orbitals, virtuals)
    denominator = (
        i_energy[:, :, None, None, None]
        + j_energy[:, None, None, :, None]
        - vir_energy[None, None, :, None, None]
        - vir_energy[None, None, None, None, :]
    )
    values = (2.0 * k_grid - jnp.swapaxes(k_grid, 2, 4)) / denominator
    values = values * usable[:, None, None, None, None]
    return values.astype(jnp.bfloat16).reshape(slots, orbitals * virtuals, orbitals * virtuals)


def local(integrals, occ_count, occ_energy, vir_energy, task_iblock, task_jblock):
    aux_local = integrals.shape[0]
    orbitals = integrals.shape[1]
    virtuals = integrals.shape[2]
    span = orbitals * virtuals
    block_total = lax.axis_size(OROW)
    col_total = lax.axis_size(OCOL)
    my_row = lax.axis_index(OROW)
    my_col = lax.axis_index(OCOL)
    active = jnp.arange(orbitals) < occ_count[my_row]
    masked = integrals * active.astype(jnp.bfloat16)[None, :, None]
    gathered = lax.all_gather(masked, OROW, axis=1, tiled=True)
    flat_blocks = gathered.reshape(aux_local, block_total, span)
    first_list = task_iblock[:, 0]
    task_total = first_list.shape[0]
    per_row = task_total // block_total
    task_ids = my_row * per_row + jnp.arange(per_row)
    i_block = first_list[task_ids]
    j_block = task_jblock[task_ids]
    usable = jnp.ones((per_row,), jnp.float32)
    energy_grid = occ_energy.reshape(block_total, orbitals)
    i_rows = jnp.take(flat_blocks, i_block, axis=1)
    j_rows = jnp.take(flat_blocks, j_block, axis=1)
    k_partial = jnp.einsum("psx,psy->sxy", i_rows, j_rows, preferred_element_type=jnp.float32)
    slots = k_partial.shape[0]
    i_energy = energy_grid[i_block]
    j_energy = energy_grid[j_block]
    k_total = lax.psum(k_partial, OCOL)
    amplitudes = make_amplitudes(k_total, i_energy, j_energy, vir_energy, usable)
    gamma_i = jnp.einsum("sxy,psy->psx", amplitudes, j_rows, preferred_element_type=jnp.float32)
    gamma_j = jnp.einsum("sxy,psx->psy", amplitudes, i_rows, preferred_element_type=jnp.float32)
    slice_width = span // col_total
    amp_grid = amplitudes.reshape(slots, orbitals, virtuals, span)
    column_part = lax.dynamic_slice_in_dim(amp_grid, my_col * slice_width, slice_width, 3)
    dens_part = jnp.einsum(
        "siaw,sibw->ab", column_part, column_part, preferred_element_type=jnp.float32
    )
    block_ids = jnp.arange(block_total)
    i_onehot = (i_block[:, None] == block_ids[None, :]).astype(jnp.float32)
    j_onehot = (j_block[:, None] == block_ids[None, :]).astype(jnp.float32)
    buffer = jnp.einsum(
        "sk,psx->pkx", i_onehot, gamma_i, precision=lax.Precision.HIGHEST
    ) + jnp.einsum("sk,psx->pkx", j_onehot, gamma_j, precision=lax.Precision.HIGHEST)
    owned = lax.psum_scatter(buffer, OROW, scatter_dimension=1, tiled=True)
    gamma_out = owned.reshape(aux_local, orbitals, virtuals)
    density = total_of(dens_part, OROW_OCOL, (0, 1, 2, 3)) / task_total
    return (gamma_out, density)


def solution(mesh):
    finer = Mesh(mesh.devices.reshape(4, 4, 4, 2), ("orow_0", "orow_1", "ocol_0", "ocol_1"))
    placed = (P(OCOL, OROW, None), P(), P(), P(), P(), P())
    return jax.shard_map(
        local, mesh=finer, in_specs=placed, out_specs=(P(OCOL, OROW, None), P()), check_vma=False
    )
```

profile of v0, /device:TPU:1, one launch (start us, length us, event | category | flops | bytes accessed | tf_op | source)
XLA Modules:
  0.0 520.0 jit_solution(48696897312067520)
XLA Ops:
  13.1 66.1 %all-gather.5.cloned.1.call-done = bf16[288,32,384]{2,0,1:T(8,128)(2,1)} async-done(((bf16[288,2,384]{2,0,1:T(8,128)(2,1)}), bf16[288,32,384]{2,0,1:T(8,128)(2,1)}) %all-gather.5.cloned.1.call-update) | async-done | bytes 7077904 | tf_op jit(solution)/shard_map/all_gather | solution.py:74
  79.2 8.5 %copy.47 = bf16[288,32,384]{2,1,0:T(8,128)(2,1)} copy(bf16[288,32,384]{2,0,1:T(8,128)(2,1)} %all-gather.5.cloned.1.call-done) | data formatting | bytes 14155776 | tf_op jit(solution)/shard_map/all_gather | solution.py:74
  87.8 11.3 %reshape.91 = bf16[288,16,768]{2,1,0:T(8,128)(2,1)} reshape(bf16[288,32,384]{2,1,0:T(8,128)(2,1)} %copy.47) | data formatting | bytes 14155776 | tf_op jit(solution)/shard_map/reshape | solution.py:75
  99.1 8.3 %copy.48 = bf16[288,16,768]{2,0,1:T(8,128)(2,1)} copy(bf16[288,16,768]{2,1,0:T(8,128)(2,1)} %reshape.91) | data formatting | bytes 14155776 | tf_op jit(solution)/shard_map/reshape | solution.py:75
  114.8 5.2 fusion.6
  120.0 12.5 %reshape.92 = f32[4,2,384,2,384]{4,3,2,1,0:T(2,128)} reshape(f32[4,768,768]{2,1,0:T(8,128)} %fusion.6) | data formatting | bytes 18874368 | tf_op jit(solution)/shard_map/reshape | solution.py:51
  132.5 14.8 %copy.50 = f32[4,2,384,2,384]{2,4,3,1,0:T(8,128)} copy(f32[4,2,384,2,384]{4,3,2,1,0:T(2,128)} %reshape.92) | data formatting | bytes 18874368 | tf_op jit(solution)/shard_map/reshape | solution.py:51
  157.6 103.2 %all-reduce.9.cloned.1.call-done = f32[4,2,384,2,384]{2,4,3,1,0:T(8,128)} async-done(((f32[4,2,384,2,384]{2,4,3,1,0:T(8,128)}), f32[4,2,384,2,384]{2,4,3,1,0:T(8,128)}) %all-reduce.9.cloned.1.call-update) | async-done | bytes 9437200 | tf_op jit(solution)/shard_map/psum | solution.py:90
  260.8 9.6 %copy.51 = f32[4,2,384,2,384]{4,2,3,1,0:T(8,128)} copy(f32[4,2,384,2,384]{2,4,3,1,0:T(8,128)} %all-reduce.9.cloned.1.call-done) | data formatting | bytes 18874368 | tf_op jit(solution)/shard_map/psum | solution.py:90
  270.4 9.6 %fusion.1 = bf16[4,2,384,2,384]{4,2,3,1,0:T(8,128)(2,1)} fusion(f32[4,2,384,2,384]{2,4,3,1,0:T(8,128)} %all-reduce.9.cloned.1.call-done, f32[4,2,384,2,384]{4,2,3,1,0:T(8,128)} %copy.51, f32[384]{0:T(512)S(1)} %copy-done.2, f32[4,2,384,2]{2,3,1,0:T(2,128)} %broadcast_subtract_fusion), kind=kLoop, calls=%fused_computation.9 | loop fusion | flops 11796480 | bytes 23619072 | tf_op jit(solution)/shard_map/convert_element_type | solution.py:60
  280.0 6.7 %copy.63 = bf16[4,2,384,2,384]{2,4,3,0,1:T(8,128)(2,1)} copy(bf16[4,2,384,2,384]{4,2,3,1,0:T(8,128)(2,1)} %fusion.1) | data formatting | bytes 9437184 | tf_op jit(solution)/shard_map/reshape;reshape | solution.py:95
  286.7 9.4 %copy.52 = bf16[4,2,384,2,384]{4,3,2,1,0:T(2,128)(2,1)} copy(bf16[4,2,384,2,384]{4,2,3,1,0:T(8,128)(2,1)} %fusion.1) | data formatting | bytes 9437184 | tf_op jit(solution)/shard_map/convert_element_type | solution.py:60
  296.1 11.4 %reshape.94 = bf16[4,768,768]{2,1,0:T(8,128)(2,1)} reshape(bf16[4,2,384,2,384]{4,3,2,1,0:T(2,128)(2,1)} %copy.52) | data formatting | bytes 9437184 | tf_op jit(solution)/shard_map/reshape | solution.py:60
  316.5 9.7 %fusion.3 = f32[288,768,16]{1,2,0:T(8,128)} fusion(f32[288,4,768]{2,0,1:T(8,128)S(1)} %convolution_bitcast_fusion.1, s32[4]{0:T(128)S(1)} %copy-done.4), kind=kOutput, calls=%fused_computation.11 | convolution fusion | flops 169869376 | bytes 17694736 | tf_op jit(solution)/shard_map/sk,psx->pkx/dot_general | solution.py:103
  329.5 25.9 %all-reduce.11.cloned.1.call-done = f32[128,3,384]{2,1,0:T(4,128)} async-done(((f32[128,3,384]{2,1,0:T(4,128)}), f32[128,3,384]{2,1,0:T(4,128)}) %all-reduce.11.cloned.1.call-update) | async-done | bytes 589840
  357.1 15.3 %add_bitcast_fusion = f32[288,16,768]{2,1,0:T(8,128)} fusion(f32[288,768,16]{1,2,0:T(8,128)} %fusion.3, f32[288,4,768]{2,0,1:T(8,128)} %convolution_bitcast_fusion, s32[4]{0:T(128)S(1)} %copy-done.6), kind=kOutput, calls=%fused_computation.6 | convolution fusion | flops 173408320 | bytes 31850512 | tf_op jit(solution)/shard_map/sk,psx->pkx/dot_general | solution.py:105
  372.4 18.3 %copy.55 = f32[288,16,768]{2,0,1:T(8,128)} copy(f32[288,16,768]{2,1,0:T(8,128)} %add_bitcast_fusion) | data formatting | bytes 28311552 | tf_op jit(solution)/shard_map/add | solution.py:103
  394.4 5.8 %all-reduce.13.cloned.1.call-done = f32[32,3,384]{2,1,0:T(4,128)} async-done(((f32[32,3,384]{2,1,0:T(4,128)}), f32[32,3,384]{2,1,0:T(4,128)}) %all-reduce.13.cloned.1.call-update) | async-done | bytes 147472
  401.0 14.0 %all-reduce.3 = f32[8,3,384]{2,1,0:T(4,128)S(1)} all-reduce(f32[8,3,384]{2,1,0:T(4,128)S(1)} %constant_dynamic-slice_fusion.1), channel_id=8, replica_groups=mesh['orow_0'=4,'orow_1'=4,'ocol_0'=4,'ocol_1'=2] {'ocol_0'}, use_global_device_ids=true, to_apply=%region_4.6.clone | all-reduce | flops 9216 | bytes 73728
  415.0 9.2 %all-reduce.4 = f32[2,3,384]{2,1,0:T(4,128)S(1)} all-reduce(f32[2,3,384]{2,1,0:T(4,128)S(1)} %constant_dynamic-slice_fusion), channel_id=9, replica_groups=mesh['orow_0'=4,'orow_1'=4,'ocol_0'=4,'ocol_1'=2] {'ocol_1'}, use_global_device_ids=true, to_apply=%region_5.7.clone | all-reduce | flops 2304 | bytes 18432
  426.7 10.1 %all-gather = f32[8,3,384]{2,1,0:T(4,128)S(1)} all-gather(f32[2,3,384]{2,1,0:T(4,128)S(1)} %all_gather.25), channel_id=2, replica_groups=mesh['orow_0'=4,'orow_1'=4,'ocol_0'=4,'ocol_1'=2] {'ocol_0'}, dimensions={0}, use_global_device_ids=true | all-gather | bytes 46080 | tf_op jit(solution)/shard_map/all_gather | solution.py:32
  436.9 11.4 %all-gather.1 = f32[16,2,3,384]{3,1,2,0:T(2,128)S(1)} all-gather(f32[4,2,3,384]{3,1,2,0:T(2,128)S(1)} %copy.58), channel_id=3, replica_groups=mesh['orow_0'=4,'orow_1'=4,'ocol_0'=4,'ocol_1'=2] {'orow_1'}, dimensions={0}, use_global_device_ids=true | all-gather | bytes 184320 | tf_op jit(solution)/shard_map/all_gather | solution.py:32
  448.3 14.9 %all-gather.2 = f32[16,4,2,3,384]{4,1,3,2,0:T(4,128)S(1)} all-gather(f32[4,4,2,3,384]{4,1,3,2,0:T(4,128)S(1)} %copy.59), channel_id=4, replica_groups=mesh['orow_0'=4,'orow_1'=4,'ocol_0'=4,'ocol_1'=2] {'orow_0'}, dimensions={0}, use_global_device_ids=true | all-gather | bytes 737280 | tf_op jit(solution)/shard_map/all_gather | solution.py:32
  464.7 46.0 %reduce-scatter.4.cloned.1.call-done = f32[288,1,768]{2,0,1:T(8,128)} async-done(((f32[288,16,768]{2,0,1:T(8,128)}), f32[288,1,768]{2,0,1:T(8,128)}) %reduce-scatter.4.cloned.1.call-update) | async-done | bytes 884752
  (77 shorter events, 46.6 us)
Async XLA Ops:
  7.2 4.0 copy-start
  7.2 72.1 %all-gather.5.cloned.1.call-start = ((), (), s32[]{:S(2)}) async-start(), calls=%async_computation.1 | async-start | bytes 7520256 | tf_op jit(solution)/shard_map/all_gather | solution.py:74
  11.0 249.8 %all-reduce.9.cloned.1.call-start = ((), (), s32[]{:S(2)}) async-start(), calls=%async_computation.2 | async-start | bytes 18874368 | tf_op jit(solution)/shard_map/psum | solution.py:90
  11.8 76.0 %copy-start.3 = (s32[4]{0:T(128)}, s32[4]{0:T(128)S(1)}, u32[]{:S(2)}) copy-start(s32[4]{0:T(128)S(1)} %gather_fusion.1) | copy-start | bytes 52
  13.1 74.7 %copy-start.5 = (s32[4]{0:T(128)}, s32[4]{0:T(128)S(1)}, u32[]{:S(2)}) copy-start(s32[4]{0:T(128)S(1)} %gather_fusion) | copy-start | bytes 52
  147.3 208.0 %all-reduce.11.cloned.1.call-start = ((), (), s32[]{:S(2)}) async-start(), calls=%async_computation.3 | async-start | bytes 1572864
  157.6 112.8 %copy-start.2 = (f32[384]{0:T(512)S(1)}, f32[384]{0:T(512)}, u32[]{:S(2)}) copy-start(f32[384]{0:T(512)} %param.11) | copy-start | bytes 4612
  312.3 4.2 copy-start.4
  312.3 87.9 %all-reduce.13.cloned.1.call-start = ((), (), s32[]{:S(2)}) async-start(), calls=%async_computation.4 | async-start | bytes 393216
  312.5 13.7 %slice-start = ((s8[4718592]{0:T(1024)(128)(4,1)}), s8[524288]{0:T(1024)(128)(4,1)S(1)}, s32[]{:S(2)}) async-start(s8[4718592]{0:T(1024)(128)(4,1)} %bitcast.58), calls=%async_computation.6 | async-start | bytes 1048576
  316.5 9.7 %slice-start.1 = ((s8[4718592]{0:T(1024)(128)(4,1)}), s8[4194304]{0:T(1024)(128)(4,1)S(1)}, s32[]{:S(2)}) async-start(s8[4718592]{0:T(1024)(128)(4,1)} %bitcast.58), calls=%async_computation.7 | async-start | bytes 8388608
  326.2 30.9 %copy-start.6 = (s32[4]{0:T(128)S(1)}, s32[4]{0:T(128)}, u32[]{:S(2)}) copy-start(s32[4]{0:T(128)} %copy-done.5) | copy-start | bytes 52
  357.0 153.6 %reduce-scatter.4.cloned.1.call-start = ((), (), s32[]{:S(2)}) async-start(), calls=%async_computation.5 | async-start | bytes 15040512
  390.7 0.7 copy-start.9
  390.7 1.2 copy-start.8
  390.7 1.9 copy-start.7
  391.3 121.9 %copy-start.1 = (s32[64,1]{0,1:T(1,128)S(1)}, s32[64,1]{0,1:T(1,128)}, u32[]{:S(2)}) copy-start(s32[64,1]{0,1:T(1,128)} %param.12) | copy-start | bytes 772
Sparse Core Ops, SparseCore 0:
  11.2 68.0 all-gather.4
  147.5 113.3 all-reduce.8
  312.4 42.9 all-reduce.10
  358.1 42.0 all-reduce.12
  403.6 107.0 reduce-scatter.3
where the time goes:
time: 529 us; the launch traced here: 520 us
  waiting for transfers between devices  247 us (47%)
  local copies, waits for them, and re-layouts  138 us (26%)
  blocking collectives  61.5 us (12%)
  matrix products  40 us (8%)
  other arithmetic  16.9 us (3%)
  between operations  16.2 us (3%)
    psum x1, waiting for transfers between devices, local(): k_total = lax.psum(k_partial, OCOL)  103 us
    unnamed x8, waiting for transfers between devices  77.7 us
    all_gather x1, waiting for transfers between devices, local(): gathered = lax.all_gather(masked, OROW, axis=1, tiled=True)  66.1 us
    all_gather x4, blocking collectives, gather_in_order(): pieces = lax.all_gather(pieces, axes[k])  38.2 us
    reshape x2, local copies, waits for them, and re-layouts, make_amplitudes(): k_grid = k_total.reshape(slots, orbitals, virtuals, orbitals, virtuals)  27.3 us
    unnamed x2, blocking collectives  23.3 us
    reshape x2, local copies, waits for them, and re-layouts, local(): flat_blocks = gathered.reshape(aux_local, block_total, span)  19.6 us
    add x1, local copies, waits for them, and re-layouts, local(): jnp.einsum('sk,psx->pkx', i_onehot, gamma_i, precision=lax.Precision.HIGH...  18.3 us
  transfers between devices with their start and end apart: 5, of which 5 were waited for; matrix products, arithmetic and copies ran while one was open for 13% of the time, Pallas kernels for 0%

commit v1 on v0

--- a/solution.py
+++ b/solution.py
@@ -71,7 +71,15 @@
     my_col = lax.axis_index(OCOL)
     active = jnp.arange(orbitals) < occ_count[my_row]
     masked = integrals * active.astype(jnp.bfloat16)[None, :, None]
-    gathered = lax.all_gather(masked, OROW, axis=1, tiled=True)
+    gathered = jnp.concatenate(
+        lax.all_to_all(
+            jnp.stack([masked] * lax.axis_size(OROW), axis=0),
+            axis_name=OROW,
+            split_axis=0,
+            concat_axis=0,
+        ),
+        axis=1,
+    )
     flat_blocks = gathered.reshape(aux_local, block_total, span)
     first_list = task_iblock[:, 0]
     task_total = first_list.shape[0]

time: 529 us -> 565 us (1.068)
  waiting for transfers between devices: 247 us -> 285 us
  starting transfers between devices: 0.84 us -> 9.4 us
  local copies, waits for them, and re-layouts: 138 us -> 130 us
    all_to_all x0 -> x1, waiting for transfers between devices: none -> 103 us  [local(): lax.all_to_all(jnp.stack([masked] * lax.axis_size(OROW), axis=0), axis_na...]
    all_gather x1 -> x0, waiting for transfers between devices: 66.1 us -> none  [local(): gathered = lax.all_gather(masked, OROW, axis=1, tiled=True)]
    another operation x0 -> x2, local copies, waits for them, and re-layouts: none -> 21.1 us  [the longest x1 16.1 us: local(): flat_blocks = gathered.reshape(aux_local, block_total, span)]
    reshape x2 -> x0, local copies, waits for them, and re-layouts: 19.6 us -> none  [local(): flat_blocks = gathered.reshape(aux_local, block_total, span)]
    all_to_all x0 -> x1, starting transfers between devices: none -> 8.59 us  [local(): lax.all_to_all(jnp.stack([masked] * lax.axis_size(OROW), axis=0), axis_na...]
    all_gather x1 -> x0, local copies, waits for them, and re-layouts: 8.54 us -> none  [local(): gathered = lax.all_gather(masked, OROW, axis=1, tiled=True)]
    unnamed x8 -> x7, waiting for transfers between devices: 77.7 us -> 78 us
  transfers between devices with their start and end apart: 5 -> 5, of which waited for: 5 -> 5; matrix products, arithmetic and copies ran while one was open for 13% -> 12% of each run, Pallas kernels for 0% -> 0%
where the time goes in v1:
time: 565 us; the launch traced here: 559 us
  waiting for transfers between devices  285 us (50%)
  local copies, waits for them, and re-layouts  130 us (23%)
  blocking collectives  61.5 us (11%)
  matrix products  40 us (7%)
  other arithmetic  16.4 us (3%)
  between operations  16.2 us (3%)
  starting transfers between devices  9.4 us (2%)
    psum x1, waiting for transfers between devices, local(): k_total = lax.psum(k_partial, OCOL)  105 us
    all_to_all x1, waiting for transfers between devices, local(): lax.all_to_all(jnp.stack([masked] * lax.axis_size(OROW), axis=0), axis_na...  103 us
    unnamed x7, waiting for transfers between devices  78 us
    all_gather x4, blocking collectives, gather_in_order(): pieces = lax.all_gather(pieces, axes[k])  38.2 us
    reshape x2, local copies, waits for them, and re-layouts, make_amplitudes(): k_grid = k_total.reshape(slots, orbitals, virtuals, orbitals, virtuals)  27.3 us
    unnamed x2, blocking collectives  23.3 us
    add x1, local copies, waits for them, and re-layouts, local(): jnp.einsum('sk,psx->pkx', i_onehot, gamma_i, precision=lax.Precision.HIGH...  18.3 us
    another operation x1, local copies, waits for them, and re-layouts, local(): flat_blocks = gathered.reshape(aux_local, block_total, span)  16.1 us
  transfers between devices with their start and end apart: 5, of which 5 were waited for; matrix products, arithmetic and copies ran while one was open for 12% of the time, Pallas kernels for 0%

profile of v1, /device:TPU:1, one launch (start us, length us, event | category | flops | bytes accessed | tf_op | source)
XLA Modules:
  0.0 558.7 jit_solution(9103877449518423166)
XLA Ops:
  10.5 5.0 stack.2
  15.5 8.6 %all-to-all-start = ((bf16[16,288,2,384]{3,2,1,0:T(2,128)(2,1)}), bf16[16,288,2,384]{3,2,1,0:T(2,128)(2,1)}, u32[]{:S(2)}, u32[]{:S(2)}) async-start(bf16[16,288,2,384]{3,2,1,0:T(2,128)(2,1)} %stack.2), calls=%async_computation | async-start | bytes 14155776 | tf_op jit(solution)/shard_map/all_to_all | solution.py:75
  25.5 102.6 %all-to-all-done = bf16[16,288,2,384]{3,2,1,0:T(2,128)(2,1)} async-done(((bf16[16,288,2,384]{3,2,1,0:T(2,128)(2,1)}), bf16[16,288,2,384]{3,2,1,0:T(2,128)(2,1)}, u32[]{:S(2)}, u32[]{:S(2)}) %all-to-all-start) | async-done | bytes 7077920 | tf_op jit(solution)/shard_map/all_to_all | solution.py:75
  128.2 16.1 %reshape_reshape.7 = bf16[288,16,768]{2,0,1:T(8,128)(2,1)} reshape(bf16[288,16,2,384]{3,2,0,1:T(2,128)(2,1)} %bitcast.2) | data formatting | bytes 14155776 | tf_op jit(solution)/shard_map/reshape;reshape | solution.py:83
  151.6 5.2 fusion.6
  156.8 12.5 %reshape.94 = f32[4,2,384,2,384]{4,3,2,1,0:T(2,128)} reshape(f32[4,768,768]{2,1,0:T(8,128)} %fusion.6) | data formatting | bytes 18874368 | tf_op jit(solution)/shard_map/reshape | solution.py:51
  169.4 14.8 %copy.31 = f32[4,2,384,2,384]{2,4,3,1,0:T(8,128)} copy(f32[4,2,384,2,384]{4,3,2,1,0:T(2,128)} %reshape.94) | data formatting | bytes 18874368 | tf_op jit(solution)/shard_map/reshape | solution.py:51
  194.5 104.7 %all-reduce.9.cloned.1.call-done = f32[4,2,384,2,384]{2,4,3,1,0:T(8,128)} async-done(((f32[4,2,384,2,384]{2,4,3,1,0:T(8,128)}), f32[4,2,384,2,384]{2,4,3,1,0:T(8,128)}) %all-reduce.9.cloned.1.call-update) | async-done | bytes 9437200 | tf_op jit(solution)/shard_map/psum | solution.py:98
  299.2 9.6 %copy.32 = f32[4,2,384,2,384]{4,2,3,1,0:T(8,128)} copy(f32[4,2,384,2,384]{2,4,3,1,0:T(8,128)} %all-reduce.9.cloned.1.call-done) | data formatting | bytes 18874368 | tf_op jit(solution)/shard_map/psum | solution.py:98
  308.8 9.6 %fusion.1 = bf16[4,2,384,2,384]{4,2,3,1,0:T(8,128)(2,1)} fusion(f32[4,2,384,2,384]{2,4,3,1,0:T(8,128)} %all-reduce.9.cloned.1.call-done, f32[4,2,384,2,384]{4,2,3,1,0:T(8,128)} %copy.32, f32[384]{0:T(512)S(1)} %copy-done.3, f32[4,2,384,2]{2,3,1,0:T(2,128)} %broadcast_subtract_fusion), kind=kLoop, calls=%fused_computation.9 | loop fusion | flops 11796480 | bytes 23619072 | tf_op jit(solution)/shard_map/convert_element_type | solution.py:60
  318.4 6.7 %copy.44 = bf16[4,2,384,2,384]{2,4,3,0,1:T(8,128)(2,1)} copy(bf16[4,2,384,2,384]{4,2,3,1,0:T(8,128)(2,1)} %fusion.1) | data formatting | bytes 9437184 | tf_op jit(solution)/shard_map/reshape;reshape | solution.py:103
  325.1 9.4 %copy.33 = bf16[4,2,384,2,384]{4,3,2,1,0:T(2,128)(2,1)} copy(bf16[4,2,384,2,384]{4,2,3,1,0:T(8,128)(2,1)} %fusion.1) | data formatting | bytes 9437184 | tf_op jit(solution)/shard_map/convert_element_type | solution.py:60
  334.5 11.4 %reshape.96 = bf16[4,768,768]{2,1,0:T(8,128)(2,1)} reshape(bf16[4,2,384,2,384]{4,3,2,1,0:T(2,128)(2,1)} %copy.33) | data formatting | bytes 9437184 | tf_op jit(solution)/shard_map/reshape | solution.py:60
  354.9 9.7 %fusion.3 = f32[288,768,16]{1,2,0:T(8,128)} fusion(f32[288,4,768]{2,0,1:T(8,128)S(1)} %convolution_bitcast_fusion.1, s32[4]{0:T(128)S(1)} %copy-done.5), kind=kOutput, calls=%fused_computation.11 | convolution fusion | flops 169869376 | bytes 17694736 | tf_op jit(solution)/shard_map/sk,psx->pkx/dot_general | solution.py:111
  367.9 25.9 %all-reduce.11.cloned.1.call-done = f32[128,3,384]{2,1,0:T(4,128)} async-done(((f32[128,3,384]{2,1,0:T(4,128)}), f32[128,3,384]{2,1,0:T(4,128)}) %all-reduce.11.cloned.1.call-update) | async-done | bytes 589840
  395.5 15.3 %add_bitcast_fusion = f32[288,16,768]{2,1,0:T(8,128)} fusion(f32[288,768,16]{1,2,0:T(8,128)} %fusion.3, f32[288,4,768]{2,0,1:T(8,128)} %convolution_bitcast_fusion, s32[4]{0:T(128)S(1)} %copy-done.7), kind=kOutput, calls=%fused_computation.6 | convolution fusion | flops 173408320 | bytes 31850512 | tf_op jit(solution)/shard_map/sk,psx->pkx/dot_general | solution.py:113
  410.8 18.3 %copy.36 = f32[288,16,768]{2,0,1:T(8,128)} copy(f32[288,16,768]{2,1,0:T(8,128)} %add_bitcast_fusion) | data formatting | bytes 28311552 | tf_op jit(solution)/shard_map/add | solution.py:111
  432.8 6.0 %all-reduce.13.cloned.1.call-done = f32[32,3,384]{2,1,0:T(4,128)} async-done(((f32[32,3,384]{2,1,0:T(4,128)}), f32[32,3,384]{2,1,0:T(4,128)}) %all-reduce.13.cloned.1.call-update) | async-done | bytes 147472
  439.6 14.0 %all-reduce.3 = f32[8,3,384]{2,1,0:T(4,128)S(1)} all-reduce(f32[8,3,384]{2,1,0:T(4,128)S(1)} %constant_dynamic-slice_fusion.1), channel_id=8, replica_groups=mesh['orow_0'=4,'orow_1'=4,'ocol_0'=4,'ocol_1'=2] {'ocol_0'}, use_global_device_ids=true, to_apply=%region_4.6.clone | all-reduce | flops 9216 | bytes 73728
  453.6 9.2 %all-reduce.4 = f32[2,3,384]{2,1,0:T(4,128)S(1)} all-reduce(f32[2,3,384]{2,1,0:T(4,128)S(1)} %constant_dynamic-slice_fusion), channel_id=9, replica_groups=mesh['orow_0'=4,'orow_1'=4,'ocol_0'=4,'ocol_1'=2] {'ocol_1'}, use_global_device_ids=true, to_apply=%region_5.7.clone | all-reduce | flops 2304 | bytes 18432
  465.2 10.1 %all-gather = f32[8,3,384]{2,1,0:T(4,128)S(1)} all-gather(f32[2,3,384]{2,1,0:T(4,128)S(1)} %all_gather.21), channel_id=2, replica_groups=mesh['orow_0'=4,'orow_1'=4,'ocol_0'=4,'ocol_1'=2] {'ocol_0'}, dimensions={0}, use_global_device_ids=true | all-gather | bytes 46080 | tf_op jit(solution)/shard_map/all_gather | solution.py:32
  475.4 11.3 %all-gather.1 = f32[16,2,3,384]{3,1,2,0:T(2,128)S(1)} all-gather(f32[4,2,3,384]{3,1,2,0:T(2,128)S(1)} %copy.39), channel_id=3, replica_groups=mesh['orow_0'=4,'orow_1'=4,'ocol_0'=4,'ocol_1'=2] {'orow_1'}, dimensions={0}, use_global_device_ids=true | all-gather | bytes 184320 | tf_op jit(solution)/shard_map/all_gather | solution.py:32
  486.8 14.9 %all-gather.2 = f32[16,4,2,3,384]{4,1,3,2,0:T(4,128)S(1)} all-gather(f32[4,4,2,3,384]{4,1,3,2,0:T(4,128)S(1)} %copy.40), channel_id=4, replica_groups=mesh['orow_0'=4,'orow_1'=4,'ocol_0'=4,'ocol_1'=2] {'orow_0'}, dimensions={0}, use_global_device_ids=true | all-gather | bytes 737280 | tf_op jit(solution)/shard_map/all_gather | solution.py:32
  503.3 46.1 %reduce-scatter.4.cloned.1.call-done = f32[288,1,768]{2,0,1:T(8,128)} async-done(((f32[288,16,768]{2,0,1:T(8,128)}), f32[288,1,768]{2,0,1:T(8,128)}) %reduce-scatter.4.cloned.1.call-update) | async-done | bytes 884752
  (77 shorter events, 45.5 us)
Async XLA Ops:
  7.2 17.0 %copy-start = (s32[64,1]{0,1:T(1,128)S(1)}, s32[64,1]{0,1:T(1,128)}, u32[]{:S(2)}) copy-start(s32[64,1]{0,1:T(1,128)} %param.12) | copy-start | bytes 772
  15.5 9.3 %copy-start.2 = (s32[64]{0:T(128)S(1)}, s32[64]{0:T(128)}, u32[]{:S(2)}) copy-start(s32[64]{0:T(128)} %param.13) | copy-start | bytes 772
  15.5 112.7 %all-to-all-start = ((bf16[16,288,2,384]{3,2,1,0:T(2,128)(2,1)}), bf16[16,288,2,384]{3,2,1,0:T(2,128)(2,1)}, u32[]{:S(2)}, u32[]{:S(2)}) async-start(bf16[16,288,2,384]{3,2,1,0:T(2,128)(2,1)} %stack.2), calls=%async_computation | async-start | bytes 14155776 | tf_op jit(solution)/shard_map/all_to_all | solution.py:75
  24.1 275.1 %all-reduce.9.cloned.1.call-start = ((), (), s32[]{:S(2)}) async-start(), calls=%async_computation.2 | async-start | bytes 18874368 | tf_op jit(solution)/shard_map/psum | solution.py:98
  24.8 119.4 %copy-start.4 = (s32[4]{0:T(128)}, s32[4]{0:T(128)S(1)}, u32[]{:S(2)}) copy-start(s32[4]{0:T(128)S(1)} %gather_fusion.1) | copy-start | bytes 52
  25.5 118.8 %copy-start.6 = (s32[4]{0:T(128)}, s32[4]{0:T(128)S(1)}, u32[]{:S(2)}) copy-start(s32[4]{0:T(128)S(1)} %gather_fusion) | copy-start | bytes 52
  184.2 209.6 %all-reduce.11.cloned.1.call-start = ((), (), s32[]{:S(2)}) async-start(), calls=%async_computation.3 | async-start | bytes 1572864
  194.5 114.3 %copy-start.3 = (f32[384]{0:T(512)S(1)}, f32[384]{0:T(512)}, u32[]{:S(2)}) copy-start(f32[384]{0:T(512)} %param.11) | copy-start | bytes 4612
  350.6 4.2 copy-start.5
  350.7 88.1 %all-reduce.13.cloned.1.call-start = ((), (), s32[]{:S(2)}) async-start(), calls=%async_computation.4 | async-start | bytes 393216
  350.9 13.7 %slice-start = ((s8[4718592]{0:T(1024)(128)(4,1)}), s8[524288]{0:T(1024)(128)(4,1)S(1)}, s32[]{:S(2)}) async-start(s8[4718592]{0:T(1024)(128)(4,1)} %bitcast.61), calls=%async_computation.6 | async-start | bytes 1048576
  354.9 9.7 %slice-start.1 = ((s8[4718592]{0:T(1024)(128)(4,1)}), s8[4194304]{0:T(1024)(128)(4,1)S(1)}, s32[]{:S(2)}) async-start(s8[4718592]{0:T(1024)(128)(4,1)} %bitcast.61), calls=%async_computation.7 | async-start | bytes 8388608
  364.6 30.9 %copy-start.7 = (s32[4]{0:T(128)S(1)}, s32[4]{0:T(128)}, u32[]{:S(2)}) copy-start(s32[4]{0:T(128)} %copy-done.6) | copy-start | bytes 52
  395.4 153.9 %reduce-scatter.4.cloned.1.call-start = ((), (), s32[]{:S(2)}) async-start(), calls=%async_computation.5 | async-start | bytes 15040512
  429.1 0.7 copy-start.10
  429.1 1.2 copy-start.9
  429.1 1.9 copy-start.8
  429.7 122.2 %copy-start.1 = (s32[64,1]{0,1:T(1,128)S(1)}, s32[64,1]{0,1:T(1,128)}, u32[]{:S(2)}) copy-start(s32[64,1]{0,1:T(1,128)} %param.12) | copy-start | bytes 772
Sparse Core Ops, SparseCore 0:
  184.3 114.8 all-reduce.8
  350.8 42.9 all-reduce.10
  396.7 42.0 all-reduce.12
  442.1 107.1 reduce-scatter.3
